TPU v7x, 256 devices: a whole 4x4x8 slice. The times are simulated.
256 devices in a mesh: modes: 64 (over y, x, z_hi), mom: 4 (over z_lo, core).
Axes of the slice: x: 4, y: 4, z: 8 (z_hi: 4, z_lo: 2; z = z_hi * 2 + z_lo), core: 2. Of those that a mesh axis runs over, the one named last changes fastest.
Arguments:
- elementals: float32 [2, 8, 256, 256, 256], P(None, 'mom', 'modes'), parts along dimension 1, may hold values from -64 to 64
- perambulators: float32 [64, 2, 2, 256, 256], P('modes'), may hold values from -0.25 to 0.25
- owners: int32 [2], replicated, may hold values from 0 to 63
- pairing: int32 [8], P('mom'), parts along dimension 0, may hold values from 0 to 1
Outputs:
- propagated: bfloat16 [2, 8, 2, 256, 256, 256], P(None, 'mom', None, 'modes'), parts along dimension 1
- correlator: float32 [2, 8, 2], P(None, 'mom'), parts along dimension 1
There are 4 independent parts, one for each index of `mom`. A program takes and returns all parts, laid end to end along the dimension named above; an argument that names none is the same for every part. Nothing has to cross between parts.
All inputs are finite; a program needn't handle non-finite values.
Results may differ from a plain program's by a relative error of at most 0.001.
Values sent between devices are 32-bit elements; how exact they have to be, the bound alone decides.
No kernel may reach another device: no remote copies, remote signals or barrier semaphores. Data moves between devices by JAX's collectives and lax.ppermute only.
A program may use at most 128 MiB of HBM per device.

v0:
```python
import jax
import jax.numpy as jnp
from jax import lax
from jax.sharding import PartitionSpec as P

N = 256
highest = lax.Precision.HIGHEST


def spread(block, axis, source):
    block = jnp.where(lax.axis_index(axis) == source, block, jnp.zeros_like(block))
    return lax.psum(block, axis)


def complex_product(formula, matrix_re, matrix_im, tensor_re, tensor_im):

    def single(left_part, right_part):
        return jnp.einsum(formula, left_part, right_part, precision=highest)

    real_part = single(matrix_re, tensor_re) - single(matrix_im, tensor_im)
    imag_part = single(matrix_re, tensor_im) + single(matrix_im, tensor_re)
    return (real_part, imag_part)


def local_pair(elem_re, elem_im, peram_re, peram_im):
    third_re, third_im = complex_product("kc,abc->abk", peram_re, peram_im, elem_re, elem_im)
    result = complex_product("jb,abk->kaj", peram_re, peram_im, third_re, third_im)
    return result


def shards(elementals, perambulators, owners, pairing):
    mom_count = elementals.shape[1]
    time_count = perambulators.shape[1]
    norm_scale = float(N) ** (-1.5)
    perams = []
    for time_index in range(time_count):
        perams.append(spread(perambulators[0, time_index], "modes", owners[time_index]))
    sink_slabs = []
    for mom_index in range(mom_count):
        picked = lax.dynamic_index_in_dim(elementals, pairing[mom_index], 1, keepdims=False)
        sink_slabs.append((jnp.swapaxes(picked[0], 1, 2), jnp.swapaxes(picked[1], 1, 2)))
    carried_re = [[None] * time_count for mom_index in range(mom_count)]
    carried_im = [[None] * time_count for mom_index in range(mom_count)]
    sums_real = [[None] * time_count for mom_index in range(mom_count)]
    sums_imag = [[None] * time_count for mom_index in range(mom_count)]
    for time_index in range(time_count):
        peram_re = perams[time_index][0]
        peram_im = perams[time_index][1]
        outputs = []
        for mom_index in range(mom_count):
            slab_re, slab_im = local_pair(
                elementals[0, mom_index], elementals[1, mom_index], peram_re, peram_im
            )
            outputs.append(
                complex_product(
                    "ia,kaj->kij",
                    peram_re,
                    peram_im,
                    lax.all_to_all(slab_re, "modes", split_axis=0, concat_axis=1, tiled=True),
                    lax.all_to_all(slab_im, "modes", split_axis=0, concat_axis=1, tiled=True),
                )
            )
        for mom_index in range(mom_count):
            out_re, out_im = outputs[mom_index]
            sink_re, sink_im = sink_slabs[mom_index]
            sums_real[mom_index][time_index] = jnp.sum(sink_re * out_re + sink_im * out_im)
            sums_imag[mom_index][time_index] = jnp.sum(sink_re * out_im - sink_im * out_re)
            carried_re[mom_index][time_index] = out_re
            carried_im[mom_index][time_index] = out_im
    partial_sums = jnp.stack(
        [
            jnp.stack([jnp.stack(row) for row in sums_real]),
            jnp.stack([jnp.stack(row) for row in sums_imag]),
        ]
    )
    correlator = lax.psum(partial_sums, "modes") * norm_scale
    propagated = jnp.stack(
        [
            jnp.stack([jnp.stack(row) for row in carried_re]),
            jnp.stack([jnp.stack(row) for row in carried_im]),
        ]
    ).astype(jnp.bfloat16)
    return (propagated, correlator)


def solution(mesh):
    placed = (
        P(None, "mom", "modes", None, None),
        P("modes", None, None, None, None),
        P(),
        P("mom"),
    )
    return jax.shard_map(
        shards,
        mesh=mesh,
        in_specs=placed,
        out_specs=(P(None, "mom", None, "modes", None, None), P(None, "mom", None)),
        check_vma=False,
    )
```

profile of v0, /device:TPU:32, one launch (start us, length us, event | category | flops | bytes accessed | tf_op | source)
XLA Modules:
  0.0 1279.1 jit_solution(18263410880325923134)
XLA Ops:
  9.8 2.3 select_bitcast_fusion.1
  12.1 742.1 %all-reduce.3.cloned.1.call-done = (f32[2,256,256]{2,1,0:T(8,128)}, f32[2,256,256]{2,1,0:T(8,128)}) async-done(((f32[2,256,256]{2,1,0:T(8,128)}, f32[2,256,256]{2,1,0:T(8,128)}), (f32[2,256,256]{2,1,0:T(8,128)}, f32[2,256,256]{2,1,0:T(8,128)})) %all-reduce.3.cloned.1.call-update) | async-done | bytes 1048592 | tf_op jit(solution)/shard_map/psum | solution.py:12
  754.2 2.5 fusion.23
  756.7 2.4 fusion.16
  764.9 9.8 all-to-all-start.6
  778.4 27.7 %all-to-all-done.6 = f32[256,4,256]{2,1,0:T(4,128)} async-done(((f32[256,4,256]{2,1,0:T(4,128)}), f32[256,4,256]{2,1,0:T(4,128)}, u32[]{:S(2)}, u32[]{:S(2)}) %all-to-all-start.6) | async-done | bytes 1048608 | tf_op jit(solution)/shard_map/all_to_all | solution.py:59
  806.1 6.7 all-to-all-start.7
  812.8 2.4 fusion.28
  815.3 2.3 fusion.35
  823.4 18.2 %all-to-all-done.7 = f32[256,4,256]{2,1,0:T(4,128)} async-done(((f32[256,4,256]{2,1,0:T(4,128)}), f32[256,4,256]{2,1,0:T(4,128)}, u32[]{:S(2)}, u32[]{:S(2)}) %all-to-all-start.7) | async-done | bytes 1048608 | tf_op jit(solution)/shard_map/all_to_all | solution.py:60
  841.6 5.5 all-to-all-start.3
  850.8 24.3 %all-to-all-done.3 = f32[256,4,256]{2,1,0:T(4,128)} async-done(((f32[256,4,256]{2,1,0:T(4,128)}), f32[256,4,256]{2,1,0:T(4,128)}, u32[]{:S(2)}, u32[]{:S(2)}) %all-to-all-start.3) | async-done | bytes 1048608 | tf_op jit(solution)/shard_map/all_to_all | solution.py:60
  875.1 7.1 all-to-all-start.2
  882.2 2.4 fusion.26
  884.6 2.3 fusion.19
  892.8 13.8 %all-to-all-done.2 = f32[256,4,256]{2,1,0:T(4,128)} async-done(((f32[256,4,256]{2,1,0:T(4,128)}), f32[256,4,256]{2,1,0:T(4,128)}, u32[]{:S(2)}, u32[]{:S(2)}) %all-to-all-start.2) | async-done | bytes 1048608 | tf_op jit(solution)/shard_map/all_to_all | solution.py:59
  906.5 6.5 all-to-all-start.4
  916.8 18.4 %all-to-all-done.4 = f32[256,4,256]{2,1,0:T(4,128)} async-done(((f32[256,4,256]{2,1,0:T(4,128)}), f32[256,4,256]{2,1,0:T(4,128)}, u32[]{:S(2)}, u32[]{:S(2)}) %all-to-all-start.4) | async-done | bytes 1048608 | tf_op jit(solution)/shard_map/all_to_all | solution.py:59
  935.2 6.5 all-to-all-start.5
  941.7 2.4 fusion.31
  944.1 2.3 fusion.38
  952.2 9.2 all-to-all-done.5
  961.5 6.9 all-to-all-start.1
  978.4 2.5 copy.62
  982.4 2.9 copy.50
  985.4 2.6 copy.51
  987.9 2.5 copy.47
  990.5 2.6 copy.48
  993.0 2.5 copy.53
  995.6 2.5 copy.54
  998.1 2.5 copy.56
  1000.7 2.5 copy.57
  1003.2 2.1 fusion.64
  1005.3 2.1 fusion.67
  1009.4 2.0 fusion.65
  1011.4 2.2 fusion.56
  1013.6 12.9 %all-to-all-start = ((f32[256,4,256]{2,1,0:T(4,128)}), f32[256,4,256]{2,1,0:T(4,128)}, u32[]{:S(2)}, u32[]{:S(2)}) async-start(f32[256,4,256]{2,1,0:T(4,128)} %copy.40), calls=%async_computation | async-start | bytes 2097152 | tf_op jit(solution)/shard_map/all_to_all | solution.py:59
  1026.5 2.5 copy.44
  1030.6 2.4 fusion.59
  1033.0 3.3 convolution_add_fusion
  1036.3 2.1 convolution_subtract_fusion
  1046.5 2.5 copy.41
  1053.7 6.5 add_reduce_fusion.3
  1060.2 2.6 maximum_bitcast_fusion.8
  1062.8 2.6 maximum_bitcast_fusion.10
  1065.4 194.2 %psum.23 = f32[2,2,2]{2,1,0:T(2,128)S(1)} all-reduce(f32[2,2,2]{2,1,0:T(2,128)S(1)} %pad_maximum_fusion.1), channel_id=1, replica_groups=mesh['modes'=64,'mom'=4] {'modes'}, use_global_device_ids=true, to_apply=%region_10.11 | all-reduce | flops 8 | bytes 64 | tf_op jit(solution)/shard_map/psum | solution.py:76
  1262.5 2.3 pad_maximum_fusion
  1264.8 7.2 copy.72
  (109 shorter events, 62.7 us)
Async XLA Ops:
  7.2 747.1 %all-reduce.3.cloned.1.call-start = ((), (), s32[]{:S(2)}) async-start(), calls=%async_computation.8 | async-start | bytes 2097152 | tf_op jit(solution)/shard_map/psum | solution.py:12
  754.2 4.9 copy-start
  754.2 4.9 copy-start.6
  764.9 41.1 %all-to-all-start.6 = ((f32[256,4,256]{2,1,0:T(4,128)}), f32[256,4,256]{2,1,0:T(4,128)}, u32[]{:S(2)}, u32[]{:S(2)}) async-start(f32[256,4,256]{2,1,0:T(4,128)} %copy.58), calls=%async_computation.6 | async-start | bytes 2097152 | tf_op jit(solution)/shard_map/all_to_all | solution.py:59
  806.1 35.5 %all-to-all-start.7 = ((f32[256,4,256]{2,1,0:T(4,128)}), f32[256,4,256]{2,1,0:T(4,128)}, u32[]{:S(2)}, u32[]{:S(2)}) async-start(f32[256,4,256]{2,1,0:T(4,128)} %copy.61), calls=%async_computation.7 | async-start | bytes 2097152 | tf_op jit(solution)/shard_map/all_to_all | solution.py:60
  812.8 4.7 copy-start.1
  841.6 33.5 %all-to-all-start.3 = ((f32[256,4,256]{2,1,0:T(4,128)}), f32[256,4,256]{2,1,0:T(4,128)}, u32[]{:S(2)}, u32[]{:S(2)}) async-start(f32[256,4,256]{2,1,0:T(4,128)} %copy.49), calls=%async_computation.3 | async-start | bytes 2097152 | tf_op jit(solution)/shard_map/all_to_all | solution.py:60
  848.1 34.1 %copy-start.5 = (f32[2,256,256]{2,1,0:T(8,128)S(1)}, f32[2,256,256]{2,1,0:T(8,128)}, u32[]{:S(2)}) copy-start(f32[2,256,256]{2,1,0:T(8,128)} %get-tuple-element.23) | copy-start | bytes 1572868
  875.1 31.5 %all-to-all-start.2 = ((f32[256,4,256]{2,1,0:T(4,128)}), f32[256,4,256]{2,1,0:T(4,128)}, u32[]{:S(2)}, u32[]{:S(2)}) async-start(f32[256,4,256]{2,1,0:T(4,128)} %copy.46), calls=%async_computation.2 | async-start | bytes 2097152 | tf_op jit(solution)/shard_map/all_to_all | solution.py:59
  882.2 4.7 copy-start.2
  906.5 28.6 %all-to-all-start.4 = ((f32[256,4,256]{2,1,0:T(4,128)}), f32[256,4,256]{2,1,0:T(4,128)}, u32[]{:S(2)}, u32[]{:S(2)}) async-start(f32[256,4,256]{2,1,0:T(4,128)} %copy.52), calls=%async_computation.4 | async-start | bytes 2097152 | tf_op jit(solution)/shard_map/all_to_all | solution.py:59
  935.2 26.3 %all-to-all-start.5 = ((f32[256,4,256]{2,1,0:T(4,128)}), f32[256,4,256]{2,1,0:T(4,128)}, u32[]{:S(2)}, u32[]{:S(2)}) async-start(f32[256,4,256]{2,1,0:T(4,128)} %copy.55), calls=%async_computation.5 | async-start | bytes 2097152 | tf_op jit(solution)/shard_map/all_to_all | solution.py:60
  941.7 4.7 copy-start.3
  949.6 18.8 %copy-start.24 = (s32[2]{0:T(128)S(1)}, s32[2]{0:T(128)}, u32[]{:S(2)}) copy-start(s32[2]{0:T(128)} %param.7) | copy-start | bytes 28
  961.5 52.1 %all-to-all-start.1 = ((f32[256,4,256]{2,1,0:T(4,128)}), f32[256,4,256]{2,1,0:T(4,128)}, u32[]{:S(2)}, u32[]{:S(2)}) async-start(f32[256,4,256]{2,1,0:T(4,128)} %copy.43), calls=%async_computation.1 | async-start | bytes 2097152 | tf_op jit(solution)/shard_map/all_to_all | solution.py:60
  982.4 20.8 %copy-start.7 = (f32[4,256,256]{1,2,0:T(8,128)}, f32[4,256,256]{1,2,0:T(8,128)S(1)}, u32[]{:S(2)}) copy-start(f32[4,256,256]{1,2,0:T(8,128)S(1)} %copy.63) | copy-start | bytes 3145732
  1003.2 4.1 copy-start.11
  1003.2 6.2 copy-start.9
  1003.2 8.2 copy-start.14
  1013.6 32.9 %all-to-all-start = ((f32[256,4,256]{2,1,0:T(4,128)}), f32[256,4,256]{2,1,0:T(4,128)}, u32[]{:S(2)}, u32[]{:S(2)}) async-start(f32[256,4,256]{2,1,0:T(4,128)} %copy.40), calls=%async_computation | async-start | bytes 2097152 | tf_op jit(solution)/shard_map/all_to_all | solution.py:59
  1030.6 5.7 copy-start.8
  1030.6 5.7 copy-start.22
  1030.6 7.8 copy-start.10
  1030.6 7.8 copy-start.21
  1036.3 4.1 copy-start.12
  1036.3 4.1 copy-start.20
  1038.4 4.0 copy-start.13
  1038.4 4.0 copy-start.19
  1040.4 4.0 copy-start.15
  1050.5 3.1 copy-start.4
  1050.5 3.1 copy-start.16
  1050.5 3.1 copy-start.17
  1050.5 3.1 copy-start.18
  1260.2 2.0 copy-start.23
Sparse Core Ops, SparseCore 0:
  12.2 741.9 all-reduce.2
where the time goes:
time: 1290 us; the launch traced here: 1280 us
  waiting for transfers between devices  854 us (66%)
  blocking collectives  194 us (15%)
  matrix products  79.3 us (6%)
  starting transfers between devices  62 us (5%)
  local copies, waits for them, and re-layouts  57.2 us (4%)
  between operations  20 us (2%)
    psum x1, waiting for transfers between devices, spread(): return lax.psum(block, axis)  742 us
    psum x1, blocking collectives, shards(): correlator = lax.psum(partial_sums, 'modes') * norm_scale  194 us
    dot_general x48, matrix products, single(): return jnp.einsum(formula, left_part, right_part, precision=highest)  79.3 us
    all_to_all x4, waiting for transfers between devices, shards(): lax.all_to_all(slab_re, 'modes', split_axis=0, concat_axis=1, tiled=True)  59.9 us
    all_to_all x4, waiting for transfers between devices, shards(): lax.all_to_all(slab_im, 'modes', split_axis=0, concat_axis=1, tiled=True)  51.7 us
    all_to_all x4, starting transfers between devices, shards(): lax.all_to_all(slab_re, 'modes', split_axis=0, concat_axis=1, tiled=True)  36.3 us
  transfers between devices with their start and end apart: 9, of which 8 were waited for; matrix products, arithmetic and copies ran while one was open for 8% of the time, Pallas kernels for 0%

commit v1 on v0

--- a/solution.py
+++ b/solution.py
@@ -9,7 +9,7 @@
 
 def spread(block, axis, source):
     block = jnp.where(lax.axis_index(axis) == source, block, jnp.zeros_like(block))
-    return lax.psum(block, axis)
+    return jnp.sum(lax.all_gather(block, axis), axis=0)
 
 
 def complex_product(formula, matrix_re, matrix_im, tensor_re, tensor_im):

time: 1290 us -> 1090 us (0.84)
  waiting for transfers between devices: 854 us -> 621 us
  other arithmetic: 12.7 us -> 36.4 us
    psum x1 -> x0, waiting for transfers between devices: 742 us -> none  [spread(): return lax.psum(block, axis)]
    all_gather x0 -> x2, waiting for transfers between devices: none -> 478 us  [spread(): return jnp.sum(lax.all_gather(block, axis), axis=0)]
    all_to_all x4, waiting for transfers between devices: 51.7 us -> 82.9 us  [shards(): lax.all_to_all(slab_im, 'modes', split_axis=0, concat_axis=1, tiled=True)]
    reduce_sum x0 -> x2, other arithmetic: none -> 23.8 us  [spread(): return jnp.sum(lax.all_gather(block, axis), axis=0)]
  transfers between devices with their start and end apart: 9 -> 10, of which waited for: 8 -> 8; matrix products, arithmetic and copies ran while one was open for 8% -> 13% of each run, Pallas kernels for 0% -> 0%
where the time goes in v1:
time: 1090 us; the launch traced here: 1080 us
  waiting for transfers between devices  621 us (57%)
  blocking collectives  190 us (17%)
  matrix products  79.4 us (7%)
  starting transfers between devices  72.7 us (7%)
  local copies, waits for them, and re-layouts  57.1 us (5%)
  other arithmetic  36.4 us (3%)
  between operations  19.8 us (2%)
    all_gather x2, waiting for transfers between devices, spread(): return jnp.sum(lax.all_gather(block, axis), axis=0)  478 us
    psum x1, blocking collectives, shards(): correlator = lax.psum(partial_sums, 'modes') * norm_scale  190 us
    all_to_all x4, waiting for transfers between devices, shards(): lax.all_to_all(slab_im, 'modes', split_axis=0, concat_axis=1, tiled=True)  82.9 us
    dot_general x48, matrix products, single(): return jnp.einsum(formula, left_part, right_part, precision=highest)  79.4 us
    all_to_all x4, waiting for transfers between devices, shards(): lax.all_to_all(slab_re, 'modes', split_axis=0, concat_axis=1, tiled=True)  59.3 us
    all_to_all x4, starting transfers between devices, shards(): lax.all_to_all(slab_re, 'modes', split_axis=0, concat_axis=1, tiled=True)  40.2 us
    all_to_all x4, starting transfers between devices, shards(): lax.all_to_all(slab_im, 'modes', split_axis=0, concat_axis=1, tiled=True)  32.4 us
    reduce_sum x2, other arithmetic, spread(): return jnp.sum(lax.all_gather(block, axis), axis=0)  23.8 us
  transfers between devices with their start and end apart: 10, of which 8 were waited for; matrix products, arithmetic and copies ran while one was open for 13% of the time, Pallas kernels for 0%

profile of v1, /device:TPU:32, one launch (start us, length us, event | category | flops | bytes accessed | tf_op | source)
XLA Modules:
  0.0 1076.3 jit_solution(13300727423249534009)
XLA Ops:
  9.8 2.3 slice_select_fusion.1
  12.9 288.0 %all-gather.7.cloned.1.call-done = f32[64,1,2,256,256]{4,3,2,1,0:T(8,128)} async-done(((f32[1,1,2,256,256]{4,3,2,1,0:T(8,128)}), f32[64,1,2,256,256]{4,3,2,1,0:T(8,128)}) %all-gather.7.cloned.1.call-update) | async-done | bytes 33554448 | tf_op jit(solution)/shard_map/all_gather | solution.py:12
  300.9 11.9 %reduce_sum.91 = f32[2,256,256]{2,1,0:T(8,128)S(1)} reduce(f32[64,1,2,256,256]{4,3,2,1,0:T(8,128)} %all-gather.7.cloned.1.call-done, f32[]{:T(128)} %constant.15.clone.1), dimensions={0,1}, to_apply=%region_1.2 | reduce | flops 8257536 | bytes 34078724 | tf_op jit(solution)/shard_map/reduce_sum | solution.py:12
  312.8 2.4 fusion.23
  315.2 2.3 fusion.16
  323.3 11.1 %all-to-all-start.6 = ((f32[256,4,256]{2,1,0:T(4,128)}), f32[256,4,256]{2,1,0:T(4,128)}, u32[]{:S(2)}, u32[]{:S(2)}) async-start(f32[256,4,256]{2,1,0:T(4,128)} %copy.58), calls=%async_computation.6 | async-start | bytes 2097152 | tf_op jit(solution)/shard_map/all_to_all | solution.py:59
  338.1 27.7 %all-to-all-done.6 = f32[256,4,256]{2,1,0:T(4,128)} async-done(((f32[256,4,256]{2,1,0:T(4,128)}), f32[256,4,256]{2,1,0:T(4,128)}, u32[]{:S(2)}, u32[]{:S(2)}) %all-to-all-start.6) | async-done | bytes 1048608 | tf_op jit(solution)/shard_map/all_to_all | solution.py:59
  365.8 13.7 %all-to-all-start.7 = ((f32[256,4,256]{2,1,0:T(4,128)}), f32[256,4,256]{2,1,0:T(4,128)}, u32[]{:S(2)}, u32[]{:S(2)}) async-start(f32[256,4,256]{2,1,0:T(4,128)} %copy.61), calls=%async_computation.7 | async-start | bytes 2097152 | tf_op jit(solution)/shard_map/all_to_all | solution.py:60
  379.5 2.4 fusion.28
  381.9 2.3 fusion.35
  390.0 35.9 %all-to-all-done.7 = f32[256,4,256]{2,1,0:T(4,128)} async-done(((f32[256,4,256]{2,1,0:T(4,128)}), f32[256,4,256]{2,1,0:T(4,128)}, u32[]{:S(2)}, u32[]{:S(2)}) %all-to-all-start.7) | async-done | bytes 1048608 | tf_op jit(solution)/shard_map/all_to_all | solution.py:60
  425.9 6.2 all-to-all-start.3
  435.8 30.5 %all-to-all-done.3 = f32[256,4,256]{2,1,0:T(4,128)} async-done(((f32[256,4,256]{2,1,0:T(4,128)}), f32[256,4,256]{2,1,0:T(4,128)}, u32[]{:S(2)}, u32[]{:S(2)}) %all-to-all-start.3) | async-done | bytes 1048608 | tf_op jit(solution)/shard_map/all_to_all | solution.py:60
  466.3 5.7 all-to-all-start.2
  471.9 190.4 %all-gather.5.cloned.1.call-done = f32[64,1,2,256,256]{4,3,2,1,0:T(8,128)} async-done(((f32[1,1,2,256,256]{4,3,2,1,0:T(8,128)}), f32[64,1,2,256,256]{4,3,2,1,0:T(8,128)}) %all-gather.5.cloned.1.call-update) | async-done | bytes 33554448 | tf_op jit(solution)/shard_map/all_gather | solution.py:12
  662.3 11.9 %reduce_sum.90 = f32[2,256,256]{2,1,0:T(8,128)S(1)} reduce(f32[64,1,2,256,256]{4,3,2,1,0:T(8,128)} %all-gather.5.cloned.1.call-done, f32[]{:T(128)} %constant.15.clone.1), dimensions={0,1}, to_apply=%region_0.1 | reduce | flops 8257536 | bytes 34078724 | tf_op jit(solution)/shard_map/reduce_sum | solution.py:12
  674.2 2.4 fusion.26
  676.7 2.3 fusion.19
  684.8 10.5 all-to-all-start.4
  699.1 26.3 %all-to-all-done.4 = f32[256,4,256]{2,1,0:T(4,128)} async-done(((f32[256,4,256]{2,1,0:T(4,128)}), f32[256,4,256]{2,1,0:T(4,128)}, u32[]{:S(2)}, u32[]{:S(2)}) %all-to-all-start.4) | async-done | bytes 1048608 | tf_op jit(solution)/shard_map/all_to_all | solution.py:59
  725.4 5.9 all-to-all-start.5
  731.3 2.4 fusion.31
  733.7 2.3 fusion.38
  741.8 16.6 %all-to-all-done.5 = f32[256,4,256]{2,1,0:T(4,128)} async-done(((f32[256,4,256]{2,1,0:T(4,128)}), f32[256,4,256]{2,1,0:T(4,128)}, u32[]{:S(2)}, u32[]{:S(2)}) %all-to-all-start.5) | async-done | bytes 1048608 | tf_op jit(solution)/shard_map/all_to_all | solution.py:60
  758.4 6.7 all-to-all-start.1
  775.0 2.5 copy.62
  779.0 2.9 copy.50
  781.9 2.5 copy.51
  784.4 2.5 copy.47
  787.0 2.5 copy.48
  789.5 2.5 copy.53
  792.0 2.5 copy.54
  794.6 2.5 copy.56
  797.1 2.6 copy.57
  807.9 2.2 fusion.56
  810.0 12.9 %all-to-all-start = ((f32[256,4,256]{2,1,0:T(4,128)}), f32[256,4,256]{2,1,0:T(4,128)}, u32[]{:S(2)}, u32[]{:S(2)}) async-start(f32[256,4,256]{2,1,0:T(4,128)} %copy.40), calls=%async_computation | async-start | bytes 2097152 | tf_op jit(solution)/shard_map/all_to_all | solution.py:59
  823.0 2.5 copy.44
  827.1 2.4 fusion.59
  829.5 3.3 convolution_add_fusion
  832.7 2.1 convolution_subtract_fusion
  842.9 5.3 all-to-all-done
  848.1 2.5 copy.41
  855.4 6.7 add_reduce_fusion.3
  862.0 2.5 maximum_bitcast_fusion.8
  864.5 2.6 maximum_bitcast_fusion.10
  867.2 189.6 %psum.7 = f32[2,2,2]{2,1,0:T(2,128)S(1)} all-reduce(f32[2,2,2]{2,1,0:T(2,128)S(1)} %pad_maximum_fusion.1), channel_id=1, replica_groups=mesh['modes'=64,'mom'=4] {'modes'}, use_global_device_ids=true, to_apply=%region_10.11 | all-reduce | flops 8 | bytes 64 | tf_op jit(solution)/shard_map/psum | solution.py:76
  1059.7 2.3 pad_maximum_fusion
  1062.0 7.2 copy.72
  (110 shorter events, 69.6 us)
Async XLA Ops:
  7.2 293.7 %all-gather.7.cloned.1.call-start = ((), (), s32[]{:S(2)}) async-start(), calls=%async_computation.9 | async-start | bytes 34078720 | tf_op jit(solution)/shard_map/all_gather | solution.py:12
  12.1 650.2 %all-gather.5.cloned.1.call-start = ((), (), s32[]{:S(2)}) async-start(), calls=%async_computation.8 | async-start | bytes 34078720 | tf_op jit(solution)/shard_map/all_gather | solution.py:12
  312.7 4.8 copy-start
  323.3 42.5 %all-to-all-start.6 = ((f32[256,4,256]{2,1,0:T(4,128)}), f32[256,4,256]{2,1,0:T(4,128)}, u32[]{:S(2)}, u32[]{:S(2)}) async-start(f32[256,4,256]{2,1,0:T(4,128)} %copy.58), calls=%async_computation.6 | async-start | bytes 2097152 | tf_op jit(solution)/shard_map/all_to_all | solution.py:59
  365.8 60.1 %all-to-all-start.7 = ((f32[256,4,256]{2,1,0:T(4,128)}), f32[256,4,256]{2,1,0:T(4,128)}, u32[]{:S(2)}, u32[]{:S(2)}) async-start(f32[256,4,256]{2,1,0:T(4,128)} %copy.61), calls=%async_computation.7 | async-start | bytes 2097152 | tf_op jit(solution)/shard_map/all_to_all | solution.py:60
  379.5 4.7 copy-start.1
  425.9 40.4 %all-to-all-start.3 = ((f32[256,4,256]{2,1,0:T(4,128)}), f32[256,4,256]{2,1,0:T(4,128)}, u32[]{:S(2)}, u32[]{:S(2)}) async-start(f32[256,4,256]{2,1,0:T(4,128)} %copy.49), calls=%async_computation.3 | async-start | bytes 2097152 | tf_op jit(solution)/shard_map/all_to_all | solution.py:60
  466.3 218.5 %all-to-all-start.2 = ((f32[256,4,256]{2,1,0:T(4,128)}), f32[256,4,256]{2,1,0:T(4,128)}, u32[]{:S(2)}, u32[]{:S(2)}) async-start(f32[256,4,256]{2,1,0:T(4,128)} %copy.46), calls=%async_computation.2 | async-start | bytes 2097152 | tf_op jit(solution)/shard_map/all_to_all | solution.py:59
  674.2 4.7 copy-start.2
  684.8 40.6 %all-to-all-start.4 = ((f32[256,4,256]{2,1,0:T(4,128)}), f32[256,4,256]{2,1,0:T(4,128)}, u32[]{:S(2)}, u32[]{:S(2)}) async-start(f32[256,4,256]{2,1,0:T(4,128)} %copy.52), calls=%async_computation.4 | async-start | bytes 2097152 | tf_op jit(solution)/shard_map/all_to_all | solution.py:59
  725.4 33.0 %all-to-all-start.5 = ((f32[256,4,256]{2,1,0:T(4,128)}), f32[256,4,256]{2,1,0:T(4,128)}, u32[]{:S(2)}, u32[]{:S(2)}) async-start(f32[256,4,256]{2,1,0:T(4,128)} %copy.55), calls=%async_computation.5 | async-start | bytes 2097152 | tf_op jit(solution)/shard_map/all_to_all | solution.py:60
  731.3 4.7 copy-start.3
  739.1 26.0 %copy-start.22 = (s32[2]{0:T(128)S(1)}, s32[2]{0:T(128)}, u32[]{:S(2)}) copy-start(s32[2]{0:T(128)} %param.7) | copy-start | bytes 28
  758.4 51.7 %all-to-all-start.1 = ((f32[256,4,256]{2,1,0:T(4,128)}), f32[256,4,256]{2,1,0:T(4,128)}, u32[]{:S(2)}, u32[]{:S(2)}) async-start(f32[256,4,256]{2,1,0:T(4,128)} %copy.43), calls=%async_computation.1 | async-start | bytes 2097152 | tf_op jit(solution)/shard_map/all_to_all | solution.py:60
  779.0 20.7 %copy-start.5 = (f32[4,256,256]{1,2,0:T(8,128)}, f32[4,256,256]{1,2,0:T(8,128)S(1)}, u32[]{:S(2)}) copy-start(f32[4,256,256]{1,2,0:T(8,128)S(1)} %copy.63) | copy-start | bytes 3145732
  799.7 4.1 copy-start.9
  799.7 6.2 copy-start.7
  799.7 8.2 copy-start.12
  810.0 38.1 %all-to-all-start = ((f32[256,4,256]{2,1,0:T(4,128)}), f32[256,4,256]{2,1,0:T(4,128)}, u32[]{:S(2)}, u32[]{:S(2)}) async-start(f32[256,4,256]{2,1,0:T(4,128)} %copy.40), calls=%async_computation | async-start | bytes 2097152 | tf_op jit(solution)/shard_map/all_to_all | solution.py:59
  827.0 5.7 copy-start.6
  827.0 5.7 copy-start.20
  827.0 7.8 copy-start.8
  827.0 7.8 copy-start.19
  832.7 4.1 copy-start.10
  832.7 4.1 copy-start.18
  834.8 4.0 copy-start.11
  834.8 4.0 copy-start.17
  836.9 4.0 copy-start.13
  852.2 3.1 copy-start.4
  852.2 3.1 copy-start.14
  852.2 3.1 copy-start.15
  852.2 3.1 copy-start.16
  1057.4 2.0 copy-start.21
Sparse Core Ops, SparseCore 0:
  12.2 288.5 all-gather.6
  304.2 358.1 all-gather.4
